TPU v7x, 32 devices: a whole 2x2x4 slice. The times are simulated.
32 devices in a mesh: row: 8 (over y, x, core), col: 4 (over z).
Axes of the slice: x: 2, y: 2, z: 4, core: 2. Of those that a mesh axis runs over, the one named last changes fastest.
Arguments:
- diag_blocks: float32 [16, 512, 512], P('row', None, 'col'), as said below
- near_blocks: float32 [16, 4, 512, 512], P('row', None, None, 'col'), may hold values from -0.1 to 0.1, as said below
- cluster_bases: float32 [16, 512, 512], P('row', 'col'), as said below
- near_ids: int32 [16, 4], P('row'), may hold values from 0 to 15, as said below
- near_count: int32 [16], P('row'), may hold values from 1 to 4
- parent_bases: float32 [8, 512, 512], P('row'), as said below
Outputs:
- leaf_diag: float32 [16, 256, 256], P('row', None, 'col')
- leaf_near: float32 [16, 4, 256, 256], P('row', None, None, 'col')
- parent_diag: float32 [8, 256, 256], P('row', None, 'col')
Inputs may be any that keep to these rules, and one draw needn't show every extreme that they name: `near_ids`: slot 0 of cluster i names its sibling: i + 2 when i // 2 is even, else i - 2. The other slots may name any cluster. For sibling clusters a and b = a + 2 (a // 2 even), near_blocks[b, 0] is the transpose of near_blocks[a, 0]. `diag_blocks`: Symmetric. `cluster_bases`: the identity plus a small full-rank perturbation. `parent_bases`: the identity plus a small full-rank perturbation.
All inputs are finite; a program needn't handle non-finite values.
Results may differ from a plain program's by a relative error of at most 0.0003.
Values sent between devices are 32-bit elements; how exact they have to be, the bound alone decides.
No kernel may reach another device: no remote copies, remote signals or barrier semaphores. Data moves between devices by JAX's collectives and lax.ppermute only.
A program may use at most 128 MiB of HBM per device.

v0:
```python
import jax
import jax.numpy as jnp
from jax import lax
from jax.sharding import PartitionSpec as P

B = 512
K = 256
NEAR = 4
highest = lax.Precision.HIGHEST


def partner(shard, axis, apart):
    return lax.ppermute(shard, axis, [(i, i ^ 1 << apart) for i in range(lax.axis_size(axis))])


def eliminate(dense, redundant):
    factor = jnp.linalg.cholesky(dense[:redundant, :redundant])
    solved = jax.scipy.linalg.cho_solve((factor, True), dense[:redundant, redundant:])
    schur = dense[redundant:, redundant:] - jnp.dot(
        dense[redundant:, :redundant], solved, precision=highest
    )
    return (solved, schur)


def per_device(diag_blocks, near_blocks, cluster_bases, near_ids, near_count, parent_bases):
    clusters = diag_blocks.shape[0]
    redundant = B - K
    column = lax.axis_index("col")
    quarter = K // lax.axis_size("col")
    own_rows = cluster_bases.shape[1]
    full_bases = lax.all_gather(cluster_bases, "col", axis=1, tiled=True)
    partial_value = jnp.einsum("cij,cjk->cik", diag_blocks, cluster_bases, precision=highest)
    summed = lax.psum(partial_value, "col")
    dense = jnp.einsum("cji,cjk->cik", full_bases, summed, precision=highest)
    solved, schur = jax.vmap(lambda single: eliminate(single, redundant))(dense)
    leaf_diag = lax.dynamic_slice_in_dim(schur, column * quarter, quarter, 2)
    flat_ids = near_ids.reshape(-1)
    shards = lax.all_gather(cluster_bases[:, :, redundant:], "row", axis=0, tiled=True)
    number = shards.shape[0]
    one_hot = (flat_ids[:, None] == jnp.arange(number, dtype=jnp.int32)[None, :]).astype(
        jnp.float32
    )
    picked = jnp.dot(one_hot, shards.reshape(number, -1), precision=highest)
    picked = picked.reshape(clusters, NEAR, own_rows, K)
    terms = jnp.einsum("cnij,cnjk->cnik", near_blocks, picked, precision=highest)
    right_part = lax.psum_scatter(terms, "col", scatter_dimension=3, tiled=True)
    moved = jnp.einsum("cji,cnjk->cnik", full_bases, right_part, precision=highest)
    coupled = moved[:, :, redundant:, :] - jnp.einsum(
        "cri,cnrk->cnik", solved, moved[:, :, :redundant, :], precision=highest
    )
    live = (jnp.arange(NEAR, dtype=jnp.int32)[None, :] < near_count[:, None]).astype(jnp.float32)
    leaf_near = coupled * live[:, :, None, None]
    halfway = clusters // 2
    parity = lax.axis_index("row") % 2
    stacked = jnp.stack([leaf_diag, leaf_near[:, 0]])
    kept = lax.dynamic_slice_in_dim(stacked, parity * halfway, halfway, 1)
    outgoing = lax.dynamic_slice_in_dim(stacked, (1 - parity) * halfway, halfway, 1)
    arrived = partner(outgoing, "row", 0)
    first_child = jnp.where(parity == 0, kept, arrived)
    second_child = jnp.where(parity == 0, arrived, kept)
    left_columns = jnp.concatenate([first_child[0], second_child[1]], axis=1)
    right_columns = jnp.concatenate([first_child[1], second_child[0]], axis=1)
    merged = jnp.concatenate([left_columns, right_columns], axis=2)
    rows_first = lax.dynamic_slice_in_dim(parent_bases, column * quarter, quarter, 1)
    rows_second = lax.dynamic_slice_in_dim(parent_bases, K + column * quarter, quarter, 1)
    chosen_rows = jnp.concatenate([rows_first, rows_second], axis=1)
    lifted = jnp.einsum("hji,hjk->hik", parent_bases, merged, precision=highest)
    parent_part = jnp.einsum("hij,hjk->hik", lifted, chosen_rows, precision=highest)
    parent_dense = lax.psum(parent_part, "col")
    parent_schur = jax.vmap(lambda single: eliminate(single, K)[1])(parent_dense)
    parent_diag = lax.dynamic_slice_in_dim(parent_schur, column * quarter, quarter, 2)
    return (leaf_diag, leaf_near, parent_diag)


def solution(mesh):
    return jax.shard_map(
        per_device,
        mesh=mesh,
        in_specs=(
            P("row", None, "col"),
            P("row", None, None, "col"),
            P("row", "col", None),
            P("row", None),
            P("row"),
            P("row", None, None),
        ),
        out_specs=(P("row", None, "col"), P("row", None, None, "col"), P("row", None, "col")),
        check_vma=False,
    )
```

profile of v0, /device:TPU:0, one launch (start us, length us, event | category | flops | bytes accessed | tf_op | source)
XLA Modules:
  0.0 401.4 jit_solution(10855884119777863552)
XLA Ops:
  8.1 1.8 slice.175
  9.9 4.4 %fusion.60 = f32[2,512,512]{2,1,0:T(8,128)} fusion(f32[2,512,128]{2,1,0:T(8,128)} %param.6, f32[2,128,512]{2,1,0:T(8,128)} %param.8), kind=kOutput, calls=%fused_computation.129 | convolution fusion | flops 805306368 | bytes 3145728 | tf_op jit(solution)/shard_map/cij,cjk->cik/dot_general | solution.py:32
  15.1 26.7 %all-gather.5.cloned.1.call-done = f32[16,128,256]{2,1,0:T(8,128)} async-done(((f32[2,128,256]{2,1,0:T(8,128)}), f32[16,128,256]{2,1,0:T(8,128)}) %all-gather.5.cloned.1.call-update) | async-done | bytes 2097168 | tf_op jit(solution)/shard_map/all_gather | solution.py:38
  41.8 3.8 fusion
  45.7 5.1 %convolution_bitcast_fusion = f32[2,4,512,256]{2,3,1,0:T(8,128)} fusion(f32[2,4,512,128]{3,2,1,0:T(8,128)S(1)} %copy-done, f32[2,4,128,256]{3,1,2,0:T(4,128)S(1)} %fusion), kind=kOutput, calls=%fused_computation.4 | convolution fusion | flops 1610612736 | bytes 7340032 | tf_op jit(solution)/shard_map/cnij,cnjk->cnik/dot_general | solution.py:45
  51.5 75.6 %all-reduce.5.cloned.1.call-done = f32[2,512,512]{2,1,0:T(8,128)} async-done(((f32[2,512,512]{2,1,0:T(8,128)}), f32[2,512,512]{2,1,0:T(8,128)}) %all-reduce.5.cloned.1.call-update) | async-done | bytes 2097168 | tf_op jit(solution)/shard_map/psum | solution.py:33
  127.1 5.7 %convolution_bitcast_fusion.1 = f32[2,512,512]{1,2,0:T(8,128)S(1)} fusion(f32[2,512,512]{2,1,0:T(8,128)} %all-reduce.5.cloned.1.call-done, f32[2,512,512]{2,1,0:T(8,128)} %all-gather.3.cloned.1.call-done), kind=kOutput, calls=%fused_computation.10 | convolution fusion | flops 3221225472 | bytes 6291456 | tf_op jit(solution)/shard_map/cji,cjk->cik/dot_general | solution.py:34
  132.8 1.3 copy-done.1
  137.3 23.9 %custom-call.40 = f32[2,128,128]{2,1,0:T(8,128)S(1)} custom-call(f32[2,128,128]{2,1,0:T(8,128)S(1)} %cholesky.239), custom_call_target="Cholesky" | custom-call | tf_op jit(solution)/shard_map/vmap(jit(cholesky))/cholesky | solution.py:17
  161.3 19.7 %custom-call.41 = f32[2,1,128,128]{2,3,1,0:T(8,128)S(1)} custom-call(f32[2,1,128,128]{3,2,1,0:T(8,128)S(1)} %select_bitcast_fusion), custom_call_target="InvertDiagBlocksLowerTriangular" | custom-call | tf_op jit(solution)/shard_map/vmap(jit(cholesky))/cholesky | solution.py:17
  180.9 1.2 constant_dynamic-update-slice_fusion.2
  182.1 1.3 convolution_subtract_fusion.3
  183.4 23.5 %custom-call.42 = f32[2,128,128]{2,1,0:T(8,128)S(1)} custom-call(f32[2,128,128]{2,1,0:T(8,128)S(1)} %convolution_subtract_fusion.3), custom_call_target="Cholesky" | custom-call | tf_op jit(solution)/shard_map/vmap(jit(cholesky))/cholesky | solution.py:17
  207.3 3.9 while.2
  208.0 1.3 bitcast_dynamic-update-slice_fusion.5
  209.9 1.3 bitcast_dynamic-update-slice_fusion.5
  211.2 39.5 %custom-call.43 = f32[2,2,128,128]{2,3,1,0:T(8,128)S(1)} custom-call(f32[2,2,128,128]{3,2,1,0:T(8,128)S(1)} %bitcast.192), custom_call_target="InvertDiagBlocksLowerTriangular" | custom-call | tf_op jit(solution)/shard_map/vmap(jit(_cho_solve))/triangular_solve | solution.py:18
  250.7 1.4 fusion.20
  252.1 1.6 convolution_subtract_fusion.1
  255.3 2.1 fusion.16
  258.4 3.9 fusion.4
  267.0 2.0 convolution_bitcast_fusion.2
  269.1 51.3 %all-reduce.7.cloned.1.call-done = f32[1,512,512]{1,2,0:T(8,128)} async-done(((f32[1,512,512]{1,2,0:T(8,128)}), f32[1,512,512]{1,2,0:T(8,128)}) %all-reduce.7.cloned.1.call-update) | async-done | bytes 1048592 | tf_op jit(solution)/shard_map/psum | solution.py:69
  320.4 1.9 fusion.59
  325.2 11.7 %custom-call.44 = f32[1,128,128]{2,1,0:T(8,128)S(1)} custom-call(f32[1,128,128]{2,1,0:T(8,128)S(1)} %cholesky.242), custom_call_target="Cholesky" | custom-call | tf_op jit(solution)/shard_map/vmap(jit(cholesky))/cholesky | solution.py:17
  337.0 10.0 %custom-call.45 = f32[1,1,128,128]{2,3,1,0:T(8,128)S(1)} custom-call(f32[1,1,128,128]{3,2,1,0:T(8,128)S(1)} %get-tuple-element.57), custom_call_target="InvertDiagBlocksLowerTriangular" | custom-call | tf_op jit(solution)/shard_map/vmap(jit(cholesky))/cholesky | solution.py:17
  349.1 11.7 %custom-call.46 = f32[1,128,128]{2,1,0:T(8,128)S(1)} custom-call(f32[1,128,128]{2,1,0:T(8,128)S(1)} %fusion.11), custom_call_target="Cholesky" | custom-call | tf_op jit(solution)/shard_map/vmap(jit(cholesky))/cholesky | solution.py:17
  364.3 5.3 %while.3 = (s32[]{:T(128)}, f32[1,256,256]{2,1,0:T(8,128)S(1)}, s32[2,2]{1,0:T(2,128)S(1)}, f32[2,1,128,128]{3,2,1,0:T(8,128)}, s32[]{:T(128)}) while((s32[]{:T(128)}, f32[1,256,256]{2,1,0:T(8,128)S(1)}, s32[2,2]{1,0:T(2,128)S(1)}, f32[2,1,128,128]{3,2,1,0:T(8,128)}, s32[]{:T(128)}) %tuple.66), condition=%wide.while_cond.1, body=%wide.while_body.1.sunk | while | flops 2 | bytes 132205 | solution.py:18
  365.0 2.0 bitcast_dynamic-update-slice_fusion.6
  367.6 2.0 bitcast_dynamic-update-slice_fusion.6
  369.6 20.5 %custom-call.47 = f32[1,2,128,128]{2,3,1,0:T(8,128)S(1)} custom-call(f32[1,2,128,128]{3,2,1,0:T(8,128)} %bitcast.193), custom_call_target="InvertDiagBlocksLowerTriangular" | custom-call | tf_op jit(solution)/shard_map/vmap(jit(_cho_solve))/triangular_solve | solution.py:18
  392.6 1.5 dynamic-slice_subtract_fusion.1
  (92 shorter events, 24.7 us)
Async XLA Ops:
  8.0 37.7 %copy-start = (f32[2,4,512,128]{3,2,1,0:T(8,128)S(1)}, f32[2,4,512,128]{3,2,1,0:T(8,128)}, u32[]{:S(2)}) copy-start(f32[2,4,512,128]{3,2,1,0:T(8,128)} %param.7) | copy-start | bytes 6291460
  8.0 33.8 %all-gather.5.cloned.1.call-start = ((), (), s32[]{:S(2)}) async-start(), calls=%async_computation.3 | async-start | bytes 2359296 | tf_op jit(solution)/shard_map/all_gather | solution.py:38
  9.9 117.2 %all-reduce.5.cloned.1.call-start = ((), (), s32[]{:S(2)}) async-start(), calls=%async_computation.1 | async-start | bytes 4194304 | tf_op jit(solution)/shard_map/psum | solution.py:33
  14.3 27.5 %copy-start.9 = (s32[2,4]{1,0:T(2,128)S(1)}, s32[2,4]{1,0:T(2,128)}, u32[]{:S(2)}) copy-start(s32[2,4]{1,0:T(2,128)} %param.9) | copy-start | bytes 100
  14.3 112.8 %all-gather.3.cloned.1.call-start = ((), (), s32[]{:S(2)}) async-start(), calls=%async_computation.2 | async-start | bytes 2621440 | tf_op jit(solution)/shard_map/all_gather | solution.py:31
  15.1 243.3 %reduce-scatter.2.cloned.1.call-start = ((), (), s32[]{:S(2)}) async-start(), calls=%async_computation.4 | async-start | bytes 5242880 | tf_op jit(solution)/shard_map/reduce_scatter | solution.py:46
  50.8 0.7 copy-start.10
  50.8 269.6 %all-reduce.7.cloned.1.call-start = ((), (), s32[]{:S(2)}) async-start(), calls=%async_computation.5 | async-start | bytes 2097152 | tf_op jit(solution)/shard_map/psum | solution.py:69
  132.8 1.3 copy-start.1
  136.4 0.8 copy-start.4
  258.3 7.0 %copy-start.5 = (f32[2,256,64]{1,2,0:T(8,128)}, f32[2,256,64]{1,2,0:T(8,128)S(1)}, u32[]{:S(2)}) copy-start(f32[2,256,64]{1,2,0:T(8,128)S(1)} %dynamic-slice_subtract_fusion) | copy-start | bytes 393220
  262.9 0.8 copy-start.7
  263.7 2.6 copy-start.3
  263.8 1.5 collective-permute-start
  322.3 67.8 %copy-start.2 = (f32[1,512,512]{1,2,0:T(8,128)S(1)}, f32[1,512,512]{1,2,0:T(8,128)}, u32[]{:S(2)}) copy-start(f32[1,512,512]{1,2,0:T(8,128)} %all-reduce.7.cloned.1.call-done) | copy-start | bytes 3145732
  324.5 0.7 copy-start.8
  361.5 1.9 copy-start.6
Sparse Core Ops, SparseCore 0:
  11.3 30.4 all-gather.4
  43.4 72.8 all-gather.2
  269.2 51.1 all-reduce.6
Sparse Core Ops, SparseCore 1:
  14.4 112.6 all-reduce.4
  129.3 75.8 reduce-scatter.1
where the time goes:
time: 410 us; the launch traced here: 401 us
  other arithmetic  169 us (41%)
  waiting for transfers between devices  155 us (38%)
  matrix products  40 us (10%)
  local copies, waits for them, and re-layouts  20.5 us (5%)
  between operations  17.1 us (4%)
    another operation x16, other arithmetic, eliminate(): factor = jnp.linalg.cholesky(dense[:redundant, :redundant])  102 us
    psum x1, waiting for transfers between devices, per_device(): summed = lax.psum(partial_value, 'col')  75.6 us
    another operation x6, other arithmetic, eliminate(): jax.scipy.linalg.cho_solve((factor, True), dense[:redundant, redundant:])  61.1 us
    psum x1, waiting for transfers between devices, per_device(): parent_dense = lax.psum(parent_part, 'col')  51.3 us
    all_gather x1, waiting for transfers between devices, per_device(): lax.all_gather(cluster_bases[:, :, redundant:], 'row', axis=0, tiled=True)  26.7 us
    another operation x12, local copies, waits for them, and re-layouts  9.11 us
  transfers between devices with their start and end apart: 6, of which 4 were waited for; matrix products, arithmetic and copies ran while one was open for 36% of the time, Pallas kernels for 0%

commit v1 on v0

--- a/solution.py
+++ b/solution.py
@@ -30,7 +30,7 @@
     own_rows = cluster_bases.shape[1]
     full_bases = lax.all_gather(cluster_bases, "col", axis=1, tiled=True)
     partial_value = jnp.einsum("cij,cjk->cik", diag_blocks, cluster_bases, precision=highest)
-    summed = lax.psum(partial_value, "col")
+    summed = lax.all_gather(partial_value, axis_name="col").sum(axis=0)
     dense = jnp.einsum("cji,cjk->cik", full_bases, summed, precision=highest)
     solved, schur = jax.vmap(lambda single: eliminate(single, redundant))(dense)
     leaf_diag = lax.dynamic_slice_in_dim(schur, column * quarter, quarter, 2)

time: 410 us -> 597 us (1.46)
  waiting for transfers between devices: 155 us -> 341 us
  other arithmetic: 169 us -> 175 us
    all_gather x0 -> x1, waiting for transfers between devices: none -> 147 us  [per_device(): summed = lax.all_gather(partial_value, axis_name='col').sum(axis=0)]
    reduce_scatter x1, waiting for transfers between devices: 0.03 us -> 77.9 us  [per_device(): right_part = lax.psum_scatter(terms, 'col', scatter_dimension=3, tiled=True)]
    psum x1 -> x0, waiting for transfers between devices: 75.6 us -> none  [per_device(): summed = lax.psum(partial_value, 'col')]
    all_gather x1, waiting for transfers between devices: 0.01 us -> 33.2 us  [per_device(): full_bases = lax.all_gather(cluster_bases, 'col', axis=1, tiled=True)]
    reduce_sum x0 -> x1, other arithmetic: none -> 6.02 us  [per_device(): summed = lax.all_gather(partial_value, axis_name='col').sum(axis=0)]
  transfers between devices with their start and end apart: 6 -> 6, of which waited for: 4 -> 6; matrix products, arithmetic and copies ran while one was open for 36% -> 3% of each run, Pallas kernels for 0% -> 0%
where the time goes in v1:
time: 597 us; the launch traced here: 592 us
  waiting for transfers between devices  341 us (57%)
  other arithmetic  175 us (29%)
  matrix products  40 us (7%)
  local copies, waits for them, and re-layouts  19 us (3%)
  between operations  16.1 us (3%)
    all_gather x1, waiting for transfers between devices, per_device(): summed = lax.all_gather(partial_value, axis_name='col').sum(axis=0)  147 us
    another operation x16, other arithmetic, eliminate(): factor = jnp.linalg.cholesky(dense[:redundant, :redundant])  102 us
    reduce_scatter x1, waiting for transfers between devices, per_device(): right_part = lax.psum_scatter(terms, 'col', scatter_dimension=3, tiled=True)  77.9 us
    another operation x6, other arithmetic, eliminate(): jax.scipy.linalg.cho_solve((factor, True), dense[:redundant, redundant:])  61.2 us
    psum x1, waiting for transfers between devices, per_device(): parent_dense = lax.psum(parent_part, 'col')  50.2 us
    all_gather x1, waiting for transfers between devices, per_device(): full_bases = lax.all_gather(cluster_bases, 'col', axis=1, tiled=True)  33.2 us
    all_gather x1, waiting for transfers between devices, per_device(): lax.all_gather(cluster_bases[:, :, redundant:], 'row', axis=0, tiled=True)  31.1 us
  transfers between devices with their start and end apart: 6, of which 6 were waited for; matrix products, arithmetic and copies ran while one was open for 3% of the time, Pallas kernels for 0%

profile of v1, /device:TPU:0, one launch (start us, length us, event | category | flops | bytes accessed | tf_op | source)
XLA Modules:
  0.0 591.9 jit_solution(2076798502497142621)
XLA Ops:
  7.2 1.8 slice.175
  9.9 31.1 %all-gather.7.cloned.1.call-done = f32[16,128,256]{2,1,0:T(8,128)} async-done(((f32[2,128,256]{2,1,0:T(8,128)}), f32[16,128,256]{2,1,0:T(8,128)}) %all-gather.7.cloned.1.call-update) | async-done | bytes 2097168 | tf_op jit(solution)/shard_map/all_gather | solution.py:38
  41.0 3.8 fusion
  44.8 5.1 convolution_bitcast_fusion
  51.2 3.1 fusion.60
  55.1 33.2 %all-gather.5.cloned.1.call-done = f32[2,512,512]{2,1,0:T(8,128)} async-done(((f32[2,128,512]{2,1,0:T(8,128)}), f32[2,512,512]{2,1,0:T(8,128)}) %all-gather.5.cloned.1.call-update) | async-done | bytes 2097168 | tf_op jit(solution)/shard_map/all_gather | solution.py:31
  88.2 77.9 %reduce-scatter.2.cloned.1.call-done = f32[2,4,512,64]{2,3,1,0:T(8,128)} async-done(((f32[2,4,512,256]{2,3,1,0:T(8,128)}), f32[2,4,512,64]{2,3,1,0:T(8,128)}) %reduce-scatter.2.cloned.1.call-update) | async-done | bytes 1048592 | tf_op jit(solution)/shard_map/reduce_scatter | solution.py:46
  166.2 4.8 fusion.4
  171.0 146.7 %all-gather.9.cloned.1.call-done = f32[8,512,512]{2,1,0:T(8,128)} async-done(((f32[2,512,512]{2,1,0:T(8,128)}), f32[8,512,512]{2,1,0:T(8,128)}) %all-gather.9.cloned.1.call-update) | async-done | bytes 8388624 | tf_op jit(solution)/shard_map/all_gather | solution.py:33
  317.8 6.0 %reduce_sum.9 = f32[2,512,512]{2,1,0:T(8,128)} reduce(f32[4,2,512,512]{3,2,1,0:T(8,128)} %bitcast.189, f32[]{:T(128)} %constant.207.clone.1), dimensions={0}, to_apply=%region_0.0 | reduce | flops 1572864 | bytes 10485764 | tf_op jit(solution)/shard_map/reduce_sum | solution.py:33
  323.8 5.7 convolution_bitcast_fusion.1
  333.9 23.6 %custom-call.40 = f32[2,128,128]{2,1,0:T(8,128)S(1)} custom-call(f32[2,128,128]{2,1,0:T(8,128)S(1)} %cholesky.239), custom_call_target="Cholesky" | custom-call | tf_op jit(solution)/shard_map/vmap(jit(cholesky))/cholesky | solution.py:17
  357.6 19.7 %custom-call.41 = f32[2,1,128,128]{2,3,1,0:T(8,128)S(1)} custom-call(f32[2,1,128,128]{3,2,1,0:T(8,128)S(1)} %select_bitcast_fusion), custom_call_target="InvertDiagBlocksLowerTriangular" | custom-call | tf_op jit(solution)/shard_map/vmap(jit(cholesky))/cholesky | solution.py:17
  379.8 23.5 %custom-call.42 = f32[2,128,128]{2,1,0:T(8,128)S(1)} custom-call(f32[2,128,128]{2,1,0:T(8,128)S(1)} %convolution_subtract_fusion.3), custom_call_target="Cholesky" | custom-call | tf_op jit(solution)/shard_map/vmap(jit(cholesky))/cholesky | solution.py:17
  403.6 3.9 while.2
  407.5 39.5 %custom-call.43 = f32[2,2,128,128]{2,3,1,0:T(8,128)S(1)} custom-call(f32[2,2,128,128]{3,2,1,0:T(8,128)S(1)} %bitcast.194), custom_call_target="InvertDiagBlocksLowerTriangular" | custom-call | tf_op jit(solution)/shard_map/vmap(jit(_cho_solve))/triangular_solve | solution.py:18
  447.1 1.4 fusion.20
  448.5 1.6 convolution_subtract_fusion.1
  451.6 2.2 fusion.16
  455.8 1.4 collective-permute-done
  458.9 2.0 convolution_bitcast_fusion.2
  461.0 50.2 %all-reduce.4.cloned.1.call-done = f32[1,512,512]{1,2,0:T(8,128)} async-done(((f32[1,512,512]{1,2,0:T(8,128)}), f32[1,512,512]{1,2,0:T(8,128)}) %all-reduce.4.cloned.1.call-update) | async-done | bytes 1048592 | tf_op jit(solution)/shard_map/psum | solution.py:69
  511.2 1.9 fusion.59
  515.9 11.7 %custom-call.44 = f32[1,128,128]{2,1,0:T(8,128)S(1)} custom-call(f32[1,128,128]{2,1,0:T(8,128)S(1)} %cholesky.242), custom_call_target="Cholesky" | custom-call | tf_op jit(solution)/shard_map/vmap(jit(cholesky))/cholesky | solution.py:17
  527.7 9.8 %custom-call.45 = f32[1,1,128,128]{2,3,1,0:T(8,128)S(1)} custom-call(f32[1,1,128,128]{3,2,1,0:T(8,128)S(1)} %get-tuple-element.57), custom_call_target="InvertDiagBlocksLowerTriangular" | custom-call | tf_op jit(solution)/shard_map/vmap(jit(cholesky))/cholesky | solution.py:17
  538.6 1.3 fusion.11
  539.9 11.7 %custom-call.46 = f32[1,128,128]{2,1,0:T(8,128)S(1)} custom-call(f32[1,128,128]{2,1,0:T(8,128)S(1)} %fusion.11), custom_call_target="Cholesky" | custom-call | tf_op jit(solution)/shard_map/vmap(jit(cholesky))/cholesky | solution.py:17
  555.4 5.1 while.3
  556.0 1.9 bitcast_dynamic-update-slice_fusion.6
  558.5 1.9 bitcast_dynamic-update-slice_fusion.6
  560.4 20.5 %custom-call.47 = f32[1,2,128,128]{2,3,1,0:T(8,128)S(1)} custom-call(f32[1,2,128,128]{3,2,1,0:T(8,128)} %bitcast.195), custom_call_target="InvertDiagBlocksLowerTriangular" | custom-call | tf_op jit(solution)/shard_map/vmap(jit(_cho_solve))/triangular_solve | solution.py:18
  583.5 1.5 dynamic-slice_subtract_fusion.1
  (97 shorter events, 29.1 us)
Async XLA Ops:
  7.2 37.7 %copy-start = (f32[2,4,512,128]{3,2,1,0:T(8,128)S(1)}, f32[2,4,512,128]{3,2,1,0:T(8,128)}, u32[]{:S(2)}) copy-start(f32[2,4,512,128]{3,2,1,0:T(8,128)} %param.7) | copy-start | bytes 6291460
  7.2 33.8 %all-gather.7.cloned.1.call-start = ((), (), s32[]{:S(2)}) async-start(), calls=%async_computation.2 | async-start | bytes 2359296 | tf_op jit(solution)/shard_map/all_gather | solution.py:38
  9.1 79.2 %all-gather.5.cloned.1.call-start = ((), (), s32[]{:S(2)}) async-start(), calls=%async_computation.1 | async-start | bytes 2621440 | tf_op jit(solution)/shard_map/all_gather | solution.py:31
  9.8 156.4 %reduce-scatter.2.cloned.1.call-start = ((), (), s32[]{:S(2)}) async-start(), calls=%async_computation.3 | async-start | bytes 5242880 | tf_op jit(solution)/shard_map/reduce_scatter | solution.py:46
  50.0 1.1 copy-start.2
  50.0 1.2 copy-start.11
  50.0 5.0 copy-start.12
  50.0 267.8 %all-gather.9.cloned.1.call-start = ((), (), s32[]{:S(2)}) async-start(), calls=%async_computation.5 | async-start | bytes 10485760 | tf_op jit(solution)/shard_map/all_gather | solution.py:33
  54.3 456.9 %all-reduce.4.cloned.1.call-start = ((), (), s32[]{:S(2)}) async-start(), calls=%async_computation.4 | async-start | bytes 2097152 | tf_op jit(solution)/shard_map/psum | solution.py:69
  329.5 1.3 copy-start.1
  333.1 0.8 copy-start.6
  450.0 3.8 copy-start.3
  451.6 4.1 copy-start.5
  454.5 1.1 copy-start.9
  455.6 5.3 copy-start.7
  455.7 1.5 collective-permute-start
  513.1 67.9 %copy-start.4 = (f32[1,512,512]{1,2,0:T(8,128)S(1)}, f32[1,512,512]{1,2,0:T(8,128)}, u32[]{:S(2)}) copy-start(f32[1,512,512]{1,2,0:T(8,128)} %all-reduce.4.cloned.1.call-done) | copy-start | bytes 3145732
  515.2 0.7 copy-start.10
  552.3 2.0 copy-start.8
Sparse Core Ops, SparseCore 0:
  10.4 30.4 all-gather.6
  42.6 45.6 all-gather.4
  90.5 75.5 reduce-scatter.1
  167.6 150.1 all-gather.8
  461.1 50.0 all-reduce.3
